TPU v7x, 32 devices: a whole 2x2x4 slice. The times are simulated.
32 devices in a mesh: dp: 2 (over y), space: 16 (over z, x, core).
Axes of the slice: x: 2, y: 2, z: 4, core: 2. Of those that a mesh axis runs over, the one named last changes fastest.
Arguments:
- volumes: bfloat16 [2, 64, 32, 4096], P('dp', 'space'), may hold values from -6 to 6
- first_filter: bfloat16 [3, 3, 3, 64, 128], replicated, may hold values from -0.15625 to 0.15625
- second_filter: bfloat16 [3, 3, 3, 128, 128], replicated, may hold values from -0.109375 to 0.109375
- upstream_grad: bfloat16 [2, 16, 8, 16, 128], P('dp', 'space'), may hold values from -0.029907227 to 0.029907227
Outputs:
- second_out: bfloat16 [2, 16, 8, 16, 128], P('dp', 'space')
- first_grad: float32 [3, 3, 3, 64, 128], P(None, None, None, None, 'space')
- second_grad: float32 [3, 3, 3, 128, 128], P(None, None, None, 'space')
All inputs are finite; a program needn't handle non-finite values.
Results may differ from a plain program's by a relative error of at most 0.01.
The roundings to bfloat16 on the way count: a program that leaves them out, or rounds other values in their place, can miss the bound.
Values may be sent and summed in bfloat16 or wider, within the bound.
A program may use at most 64 MiB of HBM per device.

v0:
```python
import jax
import jax.numpy as jnp
from jax import lax
from jax.sharding import PartitionSpec as P

SLOPE = 0.3


def passed_along(value, axis, by):
    size = lax.axis_size(axis)
    pairs = [(i, i + by) for i in range(size) if 0 <= i + by < size]
    return lax.ppermute(value, axis, pairs)


def leaky_relu(values):
    return jnp.where(values > 0, values, SLOPE * values)


def strided_conv(extended, weights):
    return lax.conv_general_dilated(
        extended,
        weights,
        (2, 2, 2),
        ((0, 0), (1, 1), (1, 1)),
        dimension_numbers=("NDHWC", "DHWIO", "NDHWC"),
        preferred_element_type=jnp.float32,
    )


def filter_grad(extended, out_grads):
    return lax.conv_general_dilated(
        extended,
        out_grads,
        (1, 1, 1),
        ((0, 0), (1, 0), (1, 0)),
        rhs_dilation=(2, 2, 2),
        dimension_numbers=("CDHWN", "IDHWO", "DHWNC"),
        preferred_element_type=jnp.float32,
    )


def input_grad(out_grads, weights):
    flipped = weights[::-1, ::-1, ::-1]
    return lax.conv_general_dilated(
        out_grads,
        flipped,
        (1, 1, 1),
        ((1, 0), (1, 2), (1, 2)),
        lhs_dilation=(2, 2, 2),
        dimension_numbers=("NDHWC", "DHWOI", "NDHWC"),
        preferred_element_type=jnp.float32,
    )


def local(volumes, first_filter, second_filter, upstream_grad):
    samples, planes, height, merged = volumes.shape
    in_channels = first_filter.shape[3]
    volume_view = volumes.reshape(samples, planes, height, merged // in_channels, in_channels)
    lower_rim = passed_along(volume_view[:, -1:], "space", 1)
    volume_ext = jnp.concatenate([lower_rim, volume_view], axis=1)
    pre_one = strided_conv(volume_ext, first_filter)
    hidden = leaky_relu(pre_one).astype(jnp.bfloat16)
    middle_plane = passed_along(hidden[:, -1:], "space", 1)
    hidden_ext = jnp.concatenate([middle_plane, hidden], axis=1)
    pre_two = strided_conv(hidden_ext, second_filter)
    second_out = leaky_relu(pre_two).astype(jnp.bfloat16)
    grad_pre_two = (upstream_grad.astype(jnp.float32) * jnp.where(pre_two > 0, 1.0, SLOPE)).astype(
        jnp.bfloat16
    )
    upper_plane = passed_along(grad_pre_two[:, :1], "space", -1)
    second_term = filter_grad(hidden_ext, grad_pre_two)
    second_grad = lax.psum_scatter(second_term, "space", scatter_dimension=3, tiled=True)
    extended = jnp.concatenate([grad_pre_two, upper_plane], axis=1)
    grad_hidden = input_grad(extended, second_filter).astype(jnp.bfloat16)
    grad_pre_one = (grad_hidden.astype(jnp.float32) * jnp.where(hidden > 0, 1.0, SLOPE)).astype(
        jnp.bfloat16
    )
    first_term = filter_grad(volume_ext, grad_pre_one)
    first_grad = lax.psum_scatter(first_term, "space", scatter_dimension=4, tiled=True)
    first_grad, second_grad = lax.psum((first_grad, second_grad), "dp")
    return (second_out, first_grad, second_grad)


def solution(mesh):
    placed = (P("dp", "space", None, None), P(), P(), P("dp", "space", None, None, None))
    return jax.shard_map(
        local,
        mesh=mesh,
        in_specs=placed,
        out_specs=(
            P("dp", "space", None, None, None),
            P(None, None, None, None, "space"),
            P(None, None, None, "space", None),
        ),
        check_vma=False,
    )
```

profile of v0, /device:TPU:0, one launch (start us, length us, event | category | flops | bytes accessed | tf_op | source)
XLA Modules:
  0.0 249.5 jit_solution(9992651133310126404)
XLA Ops:
  7.2 3.3 %reshape.9 = bf16[1,4,32,64,64]{4,3,2,1,0:T(8,128)(2,1)S(1)} reshape(bf16[1,4,32,4096]{3,2,1,0:T(8,128)(2,1)} %param.4) | data formatting | bytes 2097152 | tf_op jit(solution)/shard_map/reshape | solution.py:58
  10.6 2.4 collective-permute-start
  13.0 1.5 collective-permute-done
  15.0 1.7 copy.108
  17.4 2.1 copy.70
  19.7 1.7 compare_select_fusion.1
  21.5 0.8 pad.7.clone
  22.4 1.5 fusion.69
  24.3 9.3 %collective-permute-start.1 = (bf16[1,1,16,32,128]{4,0,3,2,1:T(2,128)(2,1)S(1)}, bf16[1,1,16,32,128]{4,0,3,2,1:T(2,128)(2,1)S(1)}, u32[]{:S(2)}, u32[]{:S(2)}) collective-permute-start(bf16[1,1,16,32,128]{4,0,3,2,1:T(2,128)(2,1)S(1)} %copy.73), channel_id=1, source_target_pairs={{0,1},{1,2},{2,3},{3,4},{4,5},{5,6},{6,7},{7,8},{8,9},{9,10},{10,1... | collective-permute-start | bytes 393224 | tf_op jit(solution)/shard_map/ppermute | solution.py:12
  33.9 4.5 %copy.87 = bf16[5,32,8,12,64,1]{4,2,5,3,1,0:T(8,128)(2,1)} copy(bf16[5,32,8,12,64,1]{4,1,3,2,0,5:T(8,128)(2,1)S(1)} %bitcast.70) | data formatting | bytes 3932160 | tf_op jit(solution)/shard_map/concatenate | solution.py:60
  38.4 1.4 copy.105
  39.8 1.4 copy.106
  41.2 4.0 %fusion.10 = (bf16[5,32,8,12,64,1]{4,2,5,3,1,0:T(8,128)(2,1)}, bf16[5,32,8,12,64,1]{4,2,5,3,1,0:T(8,128)(2,1)}) fusion(bf16[5,32,1,7,1,64]{5,3,4,1,0,2:T(8,128)(2,1)S(1)} %copy.107, bf16[5,32,1,8,11,64]{5,3,4,1,0,2:T(8,128)(2,1)S(1)} %copy.106, bf16[5,32,1,8,11,64]{5,3,4,1,0,2:T(8,128)(2,1)S(1)} %copy.105, bf16[5,32,1,7,1,64]{5,3,4,1,0,2:T(8,128)(2,1)S(1)} %copy.104), kind=kLoop, calls=%fused_computation.13 | loop fusion | flops 11796480 | bytes 7823360 | tf_op jit(solution)/shard_map/concatenate | solution.py:60
  47.6 1.3 collective-permute-start.2
  48.9 3.1 %fusion.57 = f32[3,3,3,128,128]{4,3,2,1,0:T(8,128)} fusion(bf16[1,3,16,32,128]{4,0,3,2,1:T(2,128)(2,1)S(1)} %copy_dynamic-update-slice_fusion, bf16[1,1,8,16,128]{4,2,3,1,0:T(8,128)(2,1)S(1)} %fusion.56), kind=kOutput, calls=%fused_computation.64 | convolution fusion | flops 106266624 | bytes 2195456 | tf_op jit(solution)/shard_map/conv_general_dilated | solution.py:31
  52.8 0.9 fusion.30
  53.7 6.4 %fusion.22 = f32[3,3,3,64,128]{4,3,2,1,0:T(8,128)S(1)} fusion(bf16[2,16,8,6,128,1]{4,2,5,3,1,0:T(8,128)(2,1)S(1)} %fusion.30, bf16[5,32,8,12,64,1]{4,2,5,3,1,0:T(8,128)(2,1)} %get-tuple-element.23, bf16[5,32,8,12,64,1]{4,2,5,3,1,0:T(8,128)(2,1)} %copy.87, bf16[5,32,8,12,64,1]{4,2,5,3,1,0:T(8,128)(2,1)} %get-tuple-element.24), kind=kOutput, calls=%fused_computation.27 | convolution fusion | flops 683016192 | bytes 7176192 | tf_op jit(solution)/shard_map/conv_general_dilated | solution.py:31
  60.1 2.5 %copy.95 = f32[3,3,3,64,128]{3,2,1,0,4:T(4,128)} copy(f32[3,3,3,64,128]{4,3,2,1,0:T(8,128)S(1)} %fusion.22) | data formatting | bytes 1769472 | tf_op jit(solution)/shard_map/conv_general_dilated | solution.py:31
  64.6 52.0 %reduce-scatter.2.cloned.1.call-done = f32[3,3,3,8,128]{4,3,2,1,0:T(8,128)} async-done(((f32[3,3,3,128,128]{4,3,2,1,0:T(8,128)}), f32[3,3,3,8,128]{4,3,2,1,0:T(8,128)}) %reduce-scatter.2.cloned.1.call-update) | async-done | bytes 110608 | tf_op jit(solution)/shard_map/reduce_scatter | solution.py:72
  116.6 101.7 %all-reduce.6.cloned.1.call-done = f32[3,3,3,64,128]{3,2,1,0,4:T(4,128)} async-done(((f32[3,3,3,64,128]{3,2,1,0,4:T(4,128)}), f32[3,3,3,64,128]{3,2,1,0,4:T(4,128)}) %all-reduce.6.cloned.1.call-update) | async-done | bytes 884752
  218.3 0.9 constant_dynamic-slice_fusion
  219.2 10.2 %psum.14 = f32[3,3,3,64,8]{3,2,1,0,4:T(4,128)S(1)} all-reduce(f32[3,3,3,64,8]{3,2,1,0,4:T(4,128)S(1)} %constant_dynamic-slice_fusion), channel_id=1, replica_groups=mesh['dp'=2,'space'=16] {'dp'}, use_global_device_ids=true, to_apply=%region_1.2 | all-reduce | flops 13824 | bytes 110592 | tf_op jit(solution)/shard_map/psum | solution.py:80
  230.1 11.3 %all-reduce.4.cloned.1.call-done = f32[3,3,3,8,128]{4,3,2,1,0:T(8,128)} async-done(((f32[3,3,3,8,128]{4,3,2,1,0:T(8,128)}), f32[3,3,3,8,128]{4,3,2,1,0:T(8,128)}) %all-reduce.4.cloned.1.call-update) | async-done | bytes 110608 | tf_op jit(solution)/shard_map/psum | solution.py:80
  241.4 1.5 copy.122
  (55 shorter events, 7.1 us)
Async XLA Ops:
  7.2 39.8 %copy-start = (bf16[3,3,3,128,128]{4,3,2,1,0:T(8,128)(2,1)S(1)}, bf16[3,3,3,128,128]{4,3,2,1,0:T(8,128)(2,1)}, u32[]{:S(2)}) copy-start(bf16[3,3,3,128,128]{4,3,2,1,0:T(8,128)(2,1)} %param.6) | copy-start | bytes 2654212
  7.2 109.4 %reduce-scatter.2.cloned.1.call-start = ((), (), s32[]{:S(2)}) async-start(), calls=%async_computation.1 | async-start | bytes 1880064 | tf_op jit(solution)/shard_map/reduce_scatter | solution.py:72
  10.6 3.9 %collective-permute-start = (bf16[1,1,32,64,64]{4,3,2,1,0:T(8,128)(2,1)S(1)}, bf16[1,1,32,64,64]{4,3,2,1,0:T(8,128)(2,1)S(1)}, u32[]{:S(2)}, u32[]{:S(2)}) collective-permute-start(bf16[1,1,32,64,64]{4,3,2,1,0:T(8,128)(2,1)S(1)} %slice.20), channel_id=1, source_target_pairs={{0,1},{1,2},{2,3},{3,4},{4,5},{5,6},{6,7},{7,8},{8,9},{9,10},{10,1... | collective-permute-start | bytes 786440 | tf_op jit(solution)/shard_map/ppermute | solution.py:12
  17.4 2.3 copy-start.2
  17.4 2.3 copy-start.5
  24.3 21.0 %collective-permute-start.1 = (bf16[1,1,16,32,128]{4,0,3,2,1:T(2,128)(2,1)S(1)}, bf16[1,1,16,32,128]{4,0,3,2,1:T(2,128)(2,1)S(1)}, u32[]{:S(2)}, u32[]{:S(2)}) collective-permute-start(bf16[1,1,16,32,128]{4,0,3,2,1:T(2,128)(2,1)S(1)} %copy.73), channel_id=1, source_target_pairs={{0,1},{1,2},{2,3},{3,4},{4,5},{5,6},{6,7},{7,8},{8,9},{9,10},{10,1... | collective-permute-start | bytes 393224 | tf_op jit(solution)/shard_map/ppermute | solution.py:12
  45.3 1.8 copy-start.6
  45.6 2.0 copy-start.1
  47.6 5.2 %copy-start.4 = (pred[8,6]{0,1:T(8,128)(4,1)S(1)}, pred[8,6]{0,1:T(8,128)(4,1)}, u32[]{:S(2)}) copy-start(pred[8,6]{0,1:T(8,128)(4,1)} %constant.33) | copy-start | bytes 148
  47.6 5.1 %collective-permute-start.2 = (bf16[1,1,8,16,128]{4,2,3,1,0:T(8,128)(2,1)S(1)}, bf16[1,1,8,16,128]{4,2,3,1,0:T(8,128)(2,1)S(1)}, u32[]{:S(2)}, u32[]{:S(2)}) collective-permute-start(bf16[1,1,8,16,128]{4,2,3,1,0:T(8,128)(2,1)S(1)} %fusion.56), channel_id=1, source_target_pairs={{1,0},{2,1},{3,2},{4,3},{5,4},{6,5},{7,6},{8,7},{9,8},{10,9},{11,1... | collective-permute-start | bytes 98312 | tf_op jit(solution)/shard_map/ppermute | solution.py:12
  52.1 166.2 %all-reduce.6.cloned.1.call-start = ((), (), s32[]{:S(2)}) async-start(), calls=%async_computation.3 | async-start | bytes 4718592
  60.1 2.6 %copy-start.3 = (u32[32]{0:T(128)S(1)}, u32[32]{0:T(128)}, u32[]{:S(2)}) copy-start(u32[32]{0:T(128)} %constant.37) | copy-start | bytes 388
  62.7 178.8 %all-reduce.4.cloned.1.call-start = ((), (), s32[]{:S(2)}) async-start(), calls=%async_computation.2 | async-start | bytes 221184 | tf_op jit(solution)/shard_map/psum | solution.py:80
Sparse Core Ops, SparseCore 0:
  52.2 64.3 reduce-scatter.1
  120.2 98.0 all-reduce.5
  220.5 20.8 all-reduce.3
where the time goes:
time: 250 us; the launch traced here: 249 us
  waiting for transfers between devices  167 us (67%)
  local copies, waits for them, and re-layouts  27.1 us (11%)
  between operations  14.8 us (6%)
  starting transfers between devices  13.3 us (5%)
  matrix products  12.6 us (5%)
  blocking collectives  10.2 us (4%)
  other arithmetic  4.57 us (2%)
    unnamed x4, waiting for transfers between devices  102 us
    reduce_scatter x1, waiting for transfers between devices, local(): lax.psum_scatter(second_term, 'space', scatter_dimension=3, tiled=True)  52 us
    ppermute x3, starting transfers between devices, passed_along(): return lax.ppermute(value, axis, pairs)  13 us
    psum x1, waiting for transfers between devices, local(): first_grad, second_grad = lax.psum((first_grad, second_grad), 'dp')  11.3 us
    psum x1, blocking collectives, local(): first_grad, second_grad = lax.psum((first_grad, second_grad), 'dp')  10.2 us
    unnamed x26, local copies, waits for them, and re-layouts  9.87 us
    conv_general_dilated x2, matrix products, filter_grad(): lax.conv_general_dilated(extended, out_grads, (1, 1, 1), ((0, 0), (1, 0),...  9.48 us
    concatenate x5, local copies, waits for them, and re-layouts, local(): volume_ext = jnp.concatenate([lower_rim, volume_view], axis=1)  7.49 us
  transfers between devices with their start and end apart: 6, of which 5 were waited for; matrix products, arithmetic and copies ran while one was open for 11% of the time, Pallas kernels for 0%

commit v1 on v0

v1 whole, which is shorter than its diff:
```python
import functools

import jax
import jax.numpy as jnp
from jax import lax
from jax.experimental import pallas as pl
from jax.experimental.pallas import tpu as pltpu
from jax.sharding import PartitionSpec as P

SLOPE = 0.3
F32, BF16 = jnp.float32, jnp.bfloat16
MESH = pl.DeviceIdType.MESH
GROUP = 8


def dot(lhs, rhs, contract=((1,), (0,))):
    return lax.dot_general(lhs, rhs, (contract, ((), ())), preferred_element_type=F32)


def log2(n):
    return n.bit_length() - 1


def reversed_bits(value, bits):
    return sum(((value >> k) & 1) << (bits - 1 - k) for k in range(bits))


def stages_of(spaces, samples, groups):
    group_bits, space_bits = log2(groups), log2(spaces)
    extra = space_bits - group_bits
    stages = [("space", extra + k, True) for k in range(group_bits)]
    stages += [("space", k, False) for k in range(extra)]
    stages += [("dp", k, False) for k in range(log2(samples))]
    return stages


def shift_down(values, axis=1):
    at = lax.broadcasted_iota(jnp.int32, values.shape, axis)
    return jnp.where(at == 0, 0.0, pltpu.roll(values, 1, axis))


def shift_up(values, axis=1):
    size = values.shape[axis]
    at = lax.broadcasted_iota(jnp.int32, values.shape, axis)
    return jnp.where(at == size - 1, 0.0, pltpu.roll(values, size - 1, axis))


def rows_back(values):
    return jnp.concatenate([jnp.zeros_like(values[:1]), values[:-1]], axis=0)


def rows_ahead(values):
    return jnp.concatenate([values[1:], jnp.zeros_like(values[:1])], axis=0)


def flat(values):
    return values.reshape(-1, values.shape[-1])


def slope_of(values):
    return jnp.where(values > 0, 1.0, SLOPE)


class Reduction:
    def __init__(self, stages, sums, received, sends, receives, out):
        self.stages, self.sums, self.received = stages, sums, received
        self.sends, self.receives, self.out = sends, receives, out
        self.copy = None

    def start(self, t):
        axis, bit, halves = self.stages[t]
        me = lax.axis_index(axis)
        own = (me // (1 << bit)) % 2
        partner = me + (1 - 2 * own) * (1 << bit)
        held = self.sums[t]
        count = held.shape[0]
        if halves:
            source = held.at[pl.ds((1 - own) * (count // 2), count // 2)]
        else:
            source = held
        self.copy = pltpu.make_async_remote_copy(
            src_ref=source,
            dst_ref=self.received[t],
            send_sem=self.sends.at[t],
            recv_sem=self.receives.at[t],
            device_id={axis: partner},
            device_id_type=MESH,
        )
        self.copy.start()
        self.own, self.halves = own, halves

    def finish(self, t):
        self.copy.wait()
        held = self.sums[t]
        count = held.shape[0]
        if self.halves:
            mine = held[pl.ds(self.own * (count // 2), count // 2)]
        else:
            mine = held[...]
        total = mine.astype(F32) + self.received[t][...].astype(F32)
        if t + 1 < len(self.stages):
            self.sums[t + 1][...] = total.astype(BF16)
            self.start(t + 1)
        else:
            self.out[...] = total[0]


def kernel(stages, spaces, groups, vol, w1, w2, up, second_out, out1, out2, *scratch):
    count = len(stages)
    (vol_rim, hidden_send, hidden_rim, hf, g2_send, g2_next, gf, halo_send, halo_recv) = scratch[:9]
    sums2, recv2 = scratch[9 : 9 + count], scratch[9 + count : 9 + 2 * count]
    sums1, recv1 = scratch[9 + 2 * count : 9 + 3 * count], scratch[9 + 3 * count : 9 + 4 * count]
    send2, got2, send1, got1 = scratch[9 + 4 * count :]
    red2 = Reduction(stages, sums2, recv2, send2, got2, out2)
    red1 = Reduction(stages, sums1, recv1, send1, got1, out1)
    me = lax.axis_index("space")
    first, last = me == 0, me == spaces - 1
    bits = log2(groups)

    barrier = pltpu.get_barrier_semaphore()
    for axis, bit, _ in stages:
        at = lax.axis_index(axis)
        partner = at + (1 - 2 * ((at // (1 << bit)) % 2)) * (1 << bit)
        pl.semaphore_signal(barrier, inc=1, device_id={axis: partner}, device_id_type=MESH)

    @pl.when(me > 0)
    def _():
        pl.semaphore_signal(barrier, inc=1, device_id={"space": me - 1}, device_id_type=MESH)

    @pl.when(me < spaces - 1)
    def _():
        pl.semaphore_signal(barrier, inc=1, device_id={"space": me + 1}, device_id_type=MESH)

    ends = jnp.where(first, 1, 0) + jnp.where(last, 1, 0)
    pl.semaphore_wait(barrier, len(stages) + 2 - ends)

    def halo(index, source, target, by):
        return pltpu.make_async_remote_copy(
            src_ref=source,
            dst_ref=target,
            send_sem=halo_send.at[index],
            recv_sem=halo_recv.at[index],
            device_id={"space": me + by},
            device_id_type=MESH,
        )

    vol_copy = halo(0, vol.at[vol.shape[0] - 1], vol_rim, 1)
    hidden_copy = halo(1, hidden_send, hidden_rim, 1)
    g2_copy = halo(2, g2_send, g2_next, -1)

    @pl.when(me < spaces - 1)
    def _():
        vol_copy.start()

    taps1 = []
    for ab in range(9):
        zero = jnp.zeros_like(w1[0])
        right = jnp.concatenate([w1[3 * ab + 1], w1[3 * ab + 2]], axis=0)
        left = jnp.concatenate([zero, w1[3 * ab]], axis=0)
        taps1.append(jnp.concatenate([right, left], axis=1))
    w1_all = jnp.concatenate(taps1, axis=0)

    def vol_rows(plane, b):
        at = 1 if b == 0 else b - 1
        rows = vol_rim[:, at] if plane < 0 else vol[plane, :, at]
        return flat(rows_back(rows) if b == 0 else rows)

    def first_layer(p):
        columns = jnp.concatenate(
            [vol_rows(2 * p + a - 1, b) for a in range(3) for b in range(3)], axis=1
        )
        both = dot(columns, w1_all)
        cells = w1.shape[-1]
        height, width = vol.shape[1], vol.shape[3]
        here = both[:, :cells].reshape(height, width, cells)
        left = both[:, cells:].reshape(height, width, cells)
        pre = here + shift_down(left)
        return jnp.where(pre > 0, pre, SLOPE * pre).astype(BF16)

    def keep_hidden(plane, values):
        wide = values.astype(F32)
        hf[plane] = wide.reshape(hf.shape[1:])

    hidden = first_layer(1)
    hidden_send[...] = hidden

    @pl.when(me < spaces - 1)
    def _():
        hidden_copy.start()

    keep_hidden(2, hidden)

    @pl.when(me > 0)
    def _():
        vol_copy.wait_recv()

    @pl.when(first)
    def _():
        vol_rim[...] = jnp.zeros_like(vol_rim)

    keep_hidden(1, first_layer(0))

    @pl.when(me > 0)
    def _():
        hidden_copy.wait_recv()

    @pl.when(first)
    def _():
        hidden_rim[...] = jnp.zeros_like(hidden_rim)

    keep_hidden(0, hidden_rim[...])

    half_h, half_w = hf.shape[1], hf.shape[3] // 2

    def hidden_rows(plane, b, parity):
        at = 1 if b == 0 else b - 1
        rows = hf[plane, :, at, pl.ds(parity, half_w, stride=2), :]
        return flat(rows_back(rows) if b == 0 else rows)

    even = [hidden_rows(a, b, 0) for a in range(3) for b in range(3)]
    odd = [hidden_rows(a, b, 1) for a in range(3) for b in range(3)]
    pre = dot(
        jnp.concatenate([x.astype(BF16) for ab in range(9) for x in (even[ab], odd[ab])], axis=1),
        jnp.concatenate([w2[3 * ab + c] for ab in range(9) for c in (1, 2)], axis=0),
    )
    left = dot(
        jnp.concatenate([odd[ab].astype(BF16) for ab in range(9)], axis=1),
        jnp.concatenate([w2[3 * ab] for ab in range(9)], axis=0),
    )
    cells = w2.shape[-1]
    pre = pre + flat(shift_down(left.reshape(half_h, half_w, cells)))
    second_out[...] = jnp.where(pre > 0, pre, SLOPE * pre).astype(BF16)
    g2 = (up[...].astype(F32) * slope_of(pre)).astype(BF16)
    g2_send[...] = g2.reshape(half_h, half_w, cells)

    @pl.when(me > 0)
    def _():
        g2_copy.start()

    g2_wide = g2.astype(F32).reshape(half_h, half_w, cells)
    g2_ahead = shift_up(g2_wide).astype(BF16)
    g2_both = jnp.concatenate([g2, flat(g2_ahead)], axis=1)
    terms2 = []
    for ab in range(9):
        even_t = jnp.transpose(even[ab]).astype(BF16)
        odd_t = jnp.transpose(odd[ab]).astype(BF16)
        from_odd = dot(odd_t, g2_both)
        terms2 += [from_odd[:, cells:], dot(even_t, g2), from_odd[:, :cells]]

    def store_terms(target, terms):
        for k in range(0, len(terms), 2):
            one = terms[k].reshape(groups, GROUP, -1)
            two = terms[k + 1].reshape(groups, GROUP, -1) if k + 1 < len(terms) else jnp.zeros_like(one)
            pair = jnp.concatenate([one, two], axis=1).astype(BF16)
            for g in range(groups):
                target[reversed_bits(g, bits), pl.ds(k * GROUP, 2 * GROUP), :] = pair[g]

    store_terms(sums2[0], terms2)
    red2.start(0)

    @pl.when(me < spaces - 1)
    def _():
        g2_copy.wait_recv()

    @pl.when(last)
    def _():
        g2_next[...] = jnp.zeros_like(g2_next)

    planes = [(g2.reshape(half_h, half_w, cells), g2_ahead)]
    following = g2_next[...]
    planes.append((following, shift_up(following.astype(F32)).astype(BF16)))
    choices = {}
    for plane in range(2):
        for dr in range(2):
            values = planes[plane][dr]
            choices[plane, 0, dr] = flat(values)
            choices[plane, 1, dr] = flat(rows_ahead(values))
    reach = {0: [(1, 0)], 1: [(2, 0), (0, 1)]}
    for u in range(2):
        for v in range(2):
            for w in range(2):
                members = [
                    ((a * 3 + b) * 3 + c, (plane, dq, dr))
                    for a, plane in reach[u]
                    for b, dq in reach[v]
                    for c, dr in reach[w]
                ]
                grad = dot(
                    jnp.concatenate([choices[key] for _, key in members], axis=1),
                    jnp.concatenate([w2[tap] for tap, _ in members], axis=1),
                    ((1,), (1,)),
                )
                grad = grad.astype(BF16).astype(F32).reshape(half_h, half_w, cells)
                at = hf[1 + u, :, v, pl.ds(w, half_w, stride=2), :]
                grad = (grad * slope_of(at)).astype(BF16).astype(F32)
                gf[u, :, v, pl.ds(w, half_w, stride=2), :] = grad

    red2.finish(0)

    grad = gf[...].reshape(-1, gf.shape[3], cells)
    grad_t = jnp.concatenate(
        [jnp.transpose(flat(grad)).astype(BF16), jnp.transpose(flat(shift_up(grad))).astype(BF16)],
        axis=0,
    )
    pairs1, lefts1 = [], []
    for a in range(3):
        columns = jnp.concatenate(
            [
                jnp.concatenate([vol_rows(a - 1, b), vol_rows(a + 1, b)], axis=0)
                for b in range(3)
            ],
            axis=1,
        )
        both = dot(grad_t, columns)
        lanes = vol.shape[-1]
        for b in range(3):
            part = both[:, b * lanes : (b + 1) * lanes]
            pairs1.append(part[:cells])
            lefts1.append(part[cells:])
    lane = lax.broadcasted_iota(jnp.int32, lefts1[0].shape, 1)
    half = lanes // 2
    for k in range(0, 9, 2):
        upper = lefts1[k + 1] if k + 1 < 9 else jnp.zeros_like(lefts1[k])
        pairs1.append(jnp.where(lane < half, pltpu.roll(lefts1[k], half, 1), upper))
    store_terms(sums1[0], pairs1)
    red1.start(0)
    for t in range(count):
        if t + 1 < count:
            red2.finish(t + 1)
        red1.finish(t)

    @pl.when(me < spaces - 1)
    def _():
        vol_copy.wait_send()
        hidden_copy.wait_send()

    @pl.when(me > 0)
    def _():
        g2_copy.wait_send()


def local(volumes, first_filter, second_filter, upstream_grad, spaces, samples):
    _, depth, height, merged = volumes.shape
    c0, c1 = first_filter.shape[3:]
    width = merged // c0
    vol = volumes.reshape(depth, height // 2, 2, width // 2, 2 * c0)
    w1 = first_filter.reshape(27, c0, c1)
    w2 = second_filter.reshape(27, c1, c1)
    _, _, q, r, _ = upstream_grad.shape
    up = upstream_grad.reshape(q * r, c1)
    groups = min(c1 // GROUP, spaces)
    stages = stages_of(spaces, samples, groups)
    rows2, rows1 = 28 * GROUP, 14 * GROUP

    def buffers(rows):
        sums, received, size = [], [], groups
        for _, _, halves in stages:
            sums.append(pltpu.VMEM((size, rows, c1), BF16))
            size = size // 2 if halves else size
            received.append(pltpu.VMEM((size, rows, c1), BF16))
        return sums + received

    vmem = pl.BlockSpec(memory_space=pltpu.VMEM)
    dmas = pltpu.SemaphoreType.DMA((len(stages),))
    second_out, out1, out2 = pl.pallas_call(
        functools.partial(kernel, stages, spaces, groups),
        out_shape=(
            jax.ShapeDtypeStruct((q * r, c1), BF16),
            jax.ShapeDtypeStruct((rows1, c1), F32),
            jax.ShapeDtypeStruct((rows2, c1), F32),
        ),
        in_specs=[vmem] * 4,
        out_specs=(vmem,) * 3,
        scratch_shapes=[
            pltpu.VMEM((height // 2, 2, width // 2, 2 * c0), BF16),
            pltpu.VMEM((height // 2, width // 2, c1), BF16),
            pltpu.VMEM((height // 2, width // 2, c1), BF16),
            pltpu.VMEM((3, height // 4, 2, width // 2, c1), F32),
            pltpu.VMEM((q, r, c1), BF16),
            pltpu.VMEM((q, r, c1), BF16),
            pltpu.VMEM((2, height // 4, 2, width // 2, c1), F32),
            pltpu.SemaphoreType.DMA((3,)),
            pltpu.SemaphoreType.DMA((3,)),
            *buffers(rows2),
            *buffers(rows1),
            dmas,
            dmas,
            dmas,
            dmas,
        ],
        compiler_params=pltpu.CompilerParams(
            collective_id=0, has_side_effects=True, vmem_limit_bytes=50 * 1024 * 1024
        ),
    )(vol, w1, w2, up)

    own = c1 // spaces
    start = (lax.axis_index("space") % (GROUP // own)) * own if own < GROUP else 0
    units2 = out2.reshape(28, GROUP, c1)[:27]
    units1 = out1.reshape(14, GROUP, 2, c0)
    if own < GROUP:
        units2 = lax.dynamic_slice_in_dim(units2, start, own, 1)
        units1 = lax.dynamic_slice_in_dim(units1, start, own, 1)
    second_grad = units2.reshape(3, 3, 3, own, c1)
    centre = jnp.transpose(units1[:9], (0, 2, 3, 1))
    left = jnp.transpose(units1[9:], (0, 2, 3, 1)).reshape(10, c0, own)
    left = left[:9]
    first_grad = jnp.concatenate([left[:, None], centre], axis=1).reshape(3, 3, 3, c0, own)
    return second_out.reshape(1, 1, q, r, c1), first_grad, second_grad


def solution(mesh):
    placed = (P("dp", "space", None, None), P(), P(), P("dp", "space", None, None, None))
    body = functools.partial(local, spaces=mesh.shape["space"], samples=mesh.shape["dp"])
    return jax.shard_map(
        body,
        mesh=mesh,
        in_specs=placed,
        out_specs=(
            P("dp", "space", None, None, None),
            P(None, None, None, None, "space"),
            P(None, None, None, "space", None),
        ),
        check_vma=False,
    )
```

time: 250 us -> 40.4 us (0.16)
  waiting for transfers between devices: 167 us -> 0 us
  Pallas kernels: 0 us -> 35.8 us
  local copies, waits for them, and re-layouts: 27.1 us -> 3.04 us
  between operations: 14.8 us -> 0.75 us
  starting transfers between devices: 13.3 us -> 0 us
  matrix products: 12.6 us -> 0 us
  blocking collectives: 10.2 us -> 0 us
  other arithmetic: 4.57 us -> 0.66 us
    unnamed x4 -> x0, waiting for transfers between devices: 102 us -> none
    reduce_scatter x1 -> x0, waiting for transfers between devices: 52 us -> none  [local(): lax.psum_scatter(second_term, 'space', scatter_dimension=3, tiled=True)]
    pallas_call x0 -> x1, Pallas kernels: none -> 35.8 us  [local(): pl.pallas_call(functools.partial(kernel, stages, spaces, groups), out_sha...]
    ppermute x3 -> x0, starting transfers between devices: 13 us -> none  [passed_along(): return lax.ppermute(value, axis, pairs)]
    conv_general_dilated x5 -> x0, matrix products: 12.6 us -> none  [the longest x2 9.48 us: filter_grad(): lax.conv_general_dilated(extended, out_grads, (1, 1, 1), ((0, 0), (1, 0),...]
    psum x1 -> x0, waiting for transfers between devices: 11.3 us -> none  [local(): first_grad, second_grad = lax.psum((first_grad, second_grad), 'dp')]
    psum x1 -> x0, blocking collectives: 10.2 us -> none  [local(): first_grad, second_grad = lax.psum((first_grad, second_grad), 'dp')]
    concatenate x8 -> x0, local copies, waits for them, and re-layouts: 8.14 us -> none  [the longest x5 7.49 us: local(): volume_ext = jnp.concatenate([lower_rim, volume_view], axis=1)]
  transfers between devices with their start and end apart: 6 -> 0, of which waited for: 5 -> 0; matrix products, arithmetic and copies ran while one was open for 11% -> 0% of each run, Pallas kernels for 0% -> 0%
where the time goes in v1:
time: 40.4 us; the launch traced here: 40.2 us
  Pallas kernels  35.8 us (89%)
  local copies, waits for them, and re-layouts  3.04 us (8%)
  between operations  0.75 us (2%)
  other arithmetic  0.66 us (2%)
    pallas_call x1, Pallas kernels, local(): pl.pallas_call(functools.partial(kernel, stages, spaces, groups), out_sha...  35.8 us
    unnamed x8, local copies, waits for them, and re-layouts  2.17 us

profile of v1, /device:TPU:0, one launch (start us, length us, event | category | flops | bytes accessed | tf_op | source)
XLA Modules:
  0.0 40.2 jit_solution(4329357285309634738)
XLA Ops:
  0.6 0.0 copy-start
  0.6 0.0 copy-start.1
  0.7 0.0 copy-start.2
  0.7 1.5 %copy.11 = bf16[16,8,32,128]{3,2,1,0:T(8,128)(2,1)S(1)} copy(bf16[16,8,32,128]{3,1,2,0:T(8,128)(2,1)} %bitcast.23) | data formatting | bytes 2097152
  2.2 0.0 copy-done
  2.2 0.0 copy-done.1
  2.2 0.0 copy-done.2
  2.2 35.8 %shard_map.67 = (bf16[128,128]{1,0:T(8,128)(2,1)S(1)}, f32[112,128]{1,0:T(8,128)S(1)}, f32[224,128]{1,0:T(8,128)S(1)}) custom-call(bf16[4,16,2,32,128]{4,3,2,1,0:T(8,128)(2,1)S(1)} %bitcast.18, bf16[27,64,128]{2,1,0:T(8,128)(2,1)S(1)} %bitcast.20, bf16[27,128,128]{2,1,0:T(8,128)(2,1)S(1)} %bitcast.19, bf16[128,128]{1,0:T(8,128)(2,1)S(1)} %bitcast.21), custom_call_target="tpu_custom_call" | custom-call | tf_op jit(solution)/shard_map/pallas_call | solution.py:365
  38.1 0.1 slice.20
  38.2 0.1 slice.23
  38.3 0.7 %pad_maximum_fusion = f32[3,3,3,64,8]{3,4,2,1,0:T(8,128)} fusion(f32[3,3,2,64,8]{3,4,2,1,0:T(8,128)S(1)} %bitcast.24, f32[3,3,1,64,8]{3,4,2,1,0:T(8,128)S(1)} %bitcast.27), kind=kLoop, calls=%fused_computation | loop fusion | flops 13824 | bytes 110592 | tf_op jit(solution)/shard_map/concatenate | solution.py:407
  39.0 0.7 %slice.24 = f32[216,128]{1,0:T(8,128)} slice(f32[224,128]{1,0:T(8,128)S(1)} %get-tuple-element.8), slice={[0:216], [0:128]} | slice | bytes 221184 | tf_op jit(solution)/shard_map/slice | solution.py:398
  39.6 0.6 %copy.13 = bf16[1,1,8,16,128]{4,3,2,1,0:T(8,128)(2,1)} copy(bf16[1,1,8,16,128]{4,3,2,1,0:T(8,128)(2,1)S(1)} %bitcast.22) | data formatting | bytes 65536
  (5 shorter events, 0.0 us)
Async XLA Ops:
  0.6 1.6 %copy-start = (bf16[3,3,3,128,128]{4,3,2,1,0:T(8,128)(2,1)S(1)}, bf16[3,3,3,128,128]{4,3,2,1,0:T(8,128)(2,1)}, u32[]{:S(2)}) copy-start(bf16[3,3,3,128,128]{4,3,2,1,0:T(8,128)(2,1)} %param.6) | copy-start | bytes 2654212
  0.6 1.6 %copy-start.1 = (bf16[3,3,3,64,128]{4,3,2,1,0:T(8,128)(2,1)S(1)}, bf16[3,3,3,64,128]{4,3,2,1,0:T(8,128)(2,1)}, u32[]{:S(2)}) copy-start(bf16[3,3,3,64,128]{4,3,2,1,0:T(8,128)(2,1)} %param.5) | copy-start | bytes 1327108
  0.7 1.6 %copy-start.2 = (bf16[1,1,8,16,128]{4,3,2,1,0:T(8,128)(2,1)S(1)}, bf16[1,1,8,16,128]{4,3,2,1,0:T(8,128)(2,1)}, u32[]{:S(2)}) copy-start(bf16[1,1,8,16,128]{4,3,2,1,0:T(8,128)(2,1)} %param.7) | copy-start | bytes 98308

commit v2 on v1

--- a/solution.py
+++ b/solution.py
@@ -21,17 +21,38 @@
     return n.bit_length() - 1
 
 
-def reversed_bits(value, bits):
-    return sum(((value >> k) & 1) << (bits - 1 - k) for k in range(bits))
-
-
-def stages_of(spaces, samples, groups):
-    group_bits, space_bits = log2(groups), log2(spaces)
-    extra = space_bits - group_bits
-    stages = [("space", extra + k, True) for k in range(group_bits)]
-    stages += [("space", k, False) for k in range(extra)]
-    stages += [("dp", k, False) for k in range(log2(samples))]
-    return stages
+def bits_of(spaces, groups):
+    extra = log2(spaces) - log2(groups)
+    return list(range(extra, log2(spaces))), list(range(extra))
+
+
+def straight(spaces, samples, groups):
+    halving, shared = bits_of(spaces, groups)
+    stages = [("space", k, "halve") for k in halving]
+    stages += [("space", k, "full") for k in shared]
+    return stages + [("dp", k, "full") for k in range(log2(samples))]
+
+
+def samples_early(spaces, samples, groups):
+    halving, shared = bits_of(spaces, groups)
+    stages = [("space", k, "halve") for k in halving]
+    stages.insert(1, ("dp", 0, "halve"))
+    stages += [("space", k, "full") for k in shared]
+    stages += [("dp", k, "full") for k in range(1, log2(samples))]
+    return stages + [("dp", 0, "gather")]
+
+
+def block_index(stages, group, low, sample_half):
+    index = 0
+    for axis, bit, kind in stages:
+        if kind == "halve":
+            value = (group >> (bit - low)) & 1 if axis == "space" else sample_half
+            index = 2 * index + value
+    return index
+
+
+def split_of(stages):
+    return 2 if stages[-1][2] == "gather" else 1
 
 
 def shift_down(values, axis=1):
@@ -62,22 +83,23 @@
 
 
 class Reduction:
-    def __init__(self, stages, sums, received, sends, receives, out):
-        self.stages, self.sums, self.received = stages, sums, received
-        self.sends, self.receives, self.out = sends, receives, out
+    def __init__(self, stages, scratch, out, out_row):
+        count = len(stages)
+        self.stages, self.out, self.out_row = stages, out, out_row
+        self.sums, self.received = scratch[:count], scratch[count : 2 * count]
+        self.sends, self.receives = scratch[2 * count :]
         self.copy = None
 
     def start(self, t):
-        axis, bit, halves = self.stages[t]
+        axis, bit, kind = self.stages[t]
         me = lax.axis_index(axis)
         own = (me // (1 << bit)) % 2
         partner = me + (1 - 2 * own) * (1 << bit)
         held = self.sums[t]
-        count = held.shape[0]
-        if halves:
-            source = held.at[pl.ds((1 - own) * (count // 2), count // 2)]
-        else:
-            source = held
+        source = held
+        if kind == "halve":
+            half = held.shape[0] // 2
+            source = held.at[pl.ds((1 - own) * half, half)]
         self.copy = pltpu.make_async_remote_copy(
             src_ref=source,
             dst_ref=self.received[t],
@@ -87,14 +109,21 @@
             device_id_type=MESH,
         )
         self.copy.start()
-        self.own, self.halves = own, halves
+        self.own = own
 
     def finish(self, t):
         self.copy.wait()
+        kind = self.stages[t][2]
         held = self.sums[t]
-        count = held.shape[0]
-        if self.halves:
-            mine = held[pl.ds(self.own * (count // 2), count // 2)]
+        rows = held.shape[1]
+        if kind == "gather":
+            for half, values in ((self.own, held), (1 - self.own, self.received[t])):
+                at = pl.multiple_of(self.out_row + half * rows, GROUP)
+                self.out[pl.ds(at, rows), :] = values[0].astype(F32)
+            return
+        if kind == "halve":
+            half = held.shape[0] // 2
+            mine = held[pl.ds(self.own * half, half)]
         else:
             mine = held[...]
         total = mine.astype(F32) + self.received[t][...].astype(F32)
@@ -102,23 +131,24 @@
             self.sums[t + 1][...] = total.astype(BF16)
             self.start(t + 1)
         else:
-            self.out[...] = total[0]
-
-
-def kernel(stages, spaces, groups, vol, w1, w2, up, second_out, out1, out2, *scratch):
-    count = len(stages)
-    (vol_rim, hidden_send, hidden_rim, hf, g2_send, g2_next, gf, halo_send, halo_recv) = scratch[:9]
-    sums2, recv2 = scratch[9 : 9 + count], scratch[9 + count : 9 + 2 * count]
-    sums1, recv1 = scratch[9 + 2 * count : 9 + 3 * count], scratch[9 + 3 * count : 9 + 4 * count]
-    send2, got2, send1, got1 = scratch[9 + 4 * count :]
-    red2 = Reduction(stages, sums2, recv2, send2, got2, out2)
-    red1 = Reduction(stages, sums1, recv1, send1, got1, out1)
+            self.out[pl.ds(self.out_row, rows), :] = total[0]
+
+
+def kernel(plans, spaces, groups, vol, w1, w2, up, second_out, out1, out2, *scratch):
+    (vol_rim, hidden_send, hidden_rim, hf, g2_send, g2_next, gf, sum1, halo_send, halo_recv) = scratch[:10]
+    at, streams = 10, []
+    for stages, tiles, first_tile, layer in plans:
+        used = 2 * len(stages) + 2
+        target = out2 if layer == 2 else sum1
+        streams.append(Reduction(stages, scratch[at : at + used], target, first_tile * 2 * GROUP))
+        at += used
+    low = log2(spaces) - log2(groups)
     me = lax.axis_index("space")
     first, last = me == 0, me == spaces - 1
-    bits = log2(groups)
 
     barrier = pltpu.get_barrier_semaphore()
-    for axis, bit, _ in stages:
+    partners = sorted({stage[:2] for plan in plans for stage in plan[0]})
+    for axis, bit in partners:
         at = lax.axis_index(axis)
         partner = at + (1 - 2 * ((at // (1 << bit)) % 2)) * (1 << bit)
         pl.semaphore_signal(barrier, inc=1, device_id={axis: partner}, device_id_type=MESH)
@@ -132,7 +162,7 @@
         pl.semaphore_signal(barrier, inc=1, device_id={"space": me + 1}, device_id_type=MESH)
 
     ends = jnp.where(first, 1, 0) + jnp.where(last, 1, 0)
-    pl.semaphore_wait(barrier, len(stages) + 2 - ends)
+    pl.semaphore_wait(barrier, len(partners) + 2 - ends)
 
     def halo(index, source, target, by):
         return pltpu.make_async_remote_copy(
@@ -165,13 +195,17 @@
         rows = vol_rim[:, at] if plane < 0 else vol[plane, :, at]
         return flat(rows_back(rows) if b == 0 else rows)
 
-    def first_layer(p):
+    taps_rows = 3 * vol.shape[-1]
+    cells = w1.shape[-1]
+    height, width = vol.shape[1], vol.shape[3]
+
+    def first_layer(p, planes):
         columns = jnp.concatenate(
-            [vol_rows(2 * p + a - 1, b) for a in range(3) for b in range(3)], axis=1
-        )
-        both = dot(columns, w1_all)
-        cells = w1.shape[-1]
-        height, width = vol.shape[1], vol.shape[3]
+            [vol_rows(2 * p + a - 1, b) for a in planes for b in range(3)], axis=1
+        )
+        return dot(columns, w1_all[planes[0] * taps_rows : (planes[-1] + 1) * taps_rows])
+
+    def activation(both):
         here = both[:, :cells].reshape(height, width, cells)
         left = both[:, cells:].reshape(height, width, cells)
         pre = here + shift_down(left)
@@ -181,53 +215,65 @@
         wide = values.astype(F32)
         hf[plane] = wide.reshape(hf.shape[1:])
 
-    hidden = first_layer(1)
-    hidden_send[...] = hidden
-
-    @pl.when(me < spaces - 1)
-    def _():
-        hidden_copy.start()
-
-    keep_hidden(2, hidden)
-
-    @pl.when(me > 0)
-    def _():
-        vol_copy.wait_recv()
-
-    @pl.when(first)
-    def _():
-        vol_rim[...] = jnp.zeros_like(vol_rim)
-
-    keep_hidden(1, first_layer(0))
-
-    @pl.when(me > 0)
-    def _():
-        hidden_copy.wait_recv()
-
-    @pl.when(first)
-    def _():
-        hidden_rim[...] = jnp.zeros_like(hidden_rim)
-
-    keep_hidden(0, hidden_rim[...])
-
     half_h, half_w = hf.shape[1], hf.shape[3] // 2
+    even, odd = {}, {}
 
     def hidden_rows(plane, b, parity):
         at = 1 if b == 0 else b - 1
         rows = hf[plane, :, at, pl.ds(parity, half_w, stride=2), :]
         return flat(rows_back(rows) if b == 0 else rows)
 
-    even = [hidden_rows(a, b, 0) for a in range(3) for b in range(3)]
-    odd = [hidden_rows(a, b, 1) for a in range(3) for b in range(3)]
-    pre = dot(
-        jnp.concatenate([x.astype(BF16) for ab in range(9) for x in (even[ab], odd[ab])], axis=1),
-        jnp.concatenate([w2[3 * ab + c] for ab in range(9) for c in (1, 2)], axis=0),
-    )
-    left = dot(
-        jnp.concatenate([odd[ab].astype(BF16) for ab in range(9)], axis=1),
-        jnp.concatenate([w2[3 * ab] for ab in range(9)], axis=0),
-    )
-    cells = w2.shape[-1]
+    def second_layer(a):
+        taps = range(3 * a, 3 * a + 3)
+        for ab in taps:
+            even[ab], odd[ab] = hidden_rows(a, ab - 3 * a, 0), hidden_rows(a, ab - 3 * a, 1)
+        here = dot(
+            jnp.concatenate([x.astype(BF16) for ab in taps for x in (even[ab], odd[ab])], axis=1),
+            jnp.concatenate([w2[3 * ab + c] for ab in taps for c in (1, 2)], axis=0),
+        )
+        left = dot(
+            jnp.concatenate([odd[ab].astype(BF16) for ab in taps], axis=1),
+            jnp.concatenate([w2[3 * ab] for ab in taps], axis=0),
+        )
+        for ab in taps:
+            even[ab] = jnp.transpose(even[ab]).astype(BF16)
+            odd[ab] = jnp.transpose(odd[ab]).astype(BF16)
+        return here, left
+
+    hidden = activation(first_layer(1, (0, 1, 2)))
+    hidden_send[...] = hidden
+
+    @pl.when(me < spaces - 1)
+    def _():
+        hidden_copy.start()
+
+    keep_hidden(2, hidden)
+    both = first_layer(0, (1, 2))
+    here, left = second_layer(2)
+
+    @pl.when(me > 0)
+    def _():
+        vol_copy.wait_recv()
+
+    @pl.when(first)
+    def _():
+        vol_rim[...] = jnp.zeros_like(vol_rim)
+
+    keep_hidden(1, activation(both + first_layer(0, (0,))))
+    here_1, left_1 = second_layer(1)
+
+    @pl.when(me > 0)
+    def _():
+        hidden_copy.wait_recv()
+
+    @pl.when(first)
+    def _():
+        hidden_rim[...] = jnp.zeros_like(hidden_rim)
+
+    keep_hidden(0, hidden_rim[...])
+    here_0, left_0 = second_layer(0)
+    pre = here + here_1 + here_0
+    left = left + left_1 + left_0
     pre = pre + flat(shift_down(left.reshape(half_h, half_w, cells)))
     second_out[...] = jnp.where(pre > 0, pre, SLOPE * pre).astype(BF16)
     g2 = (up[...].astype(F32) * slope_of(pre)).astype(BF16)
@@ -242,21 +288,28 @@
     g2_both = jnp.concatenate([g2, flat(g2_ahead)], axis=1)
     terms2 = []
     for ab in range(9):
-        even_t = jnp.transpose(even[ab]).astype(BF16)
-        odd_t = jnp.transpose(odd[ab]).astype(BF16)
-        from_odd = dot(odd_t, g2_both)
-        terms2 += [from_odd[:, cells:], dot(even_t, g2), from_odd[:, :cells]]
-
-    def store_terms(target, terms):
-        for k in range(0, len(terms), 2):
-            one = terms[k].reshape(groups, GROUP, -1)
-            two = terms[k + 1].reshape(groups, GROUP, -1) if k + 1 < len(terms) else jnp.zeros_like(one)
-            pair = jnp.concatenate([one, two], axis=1).astype(BF16)
-            for g in range(groups):
-                target[reversed_bits(g, bits), pl.ds(k * GROUP, 2 * GROUP), :] = pair[g]
-
-    store_terms(sums2[0], terms2)
-    red2.start(0)
+        from_odd = dot(odd[ab], g2_both)
+        terms2 += [from_odd[:, cells:], dot(even[ab], g2), from_odd[:, :cells]]
+
+    def begin(layer, terms):
+        for stream, (stages, tiles, first_tile, of) in zip(streams, plans):
+            if of != layer:
+                continue
+            share = tiles // split_of(stages)
+            for tile in range(tiles):
+                k = 2 * (first_tile + tile)
+                one = terms[k].reshape(groups, GROUP, -1)
+                two = jnp.zeros_like(one)
+                if k + 1 < len(terms):
+                    two = terms[k + 1].reshape(groups, GROUP, -1)
+                pair = jnp.concatenate([one, two], axis=1).astype(BF16)
+                rows = pl.ds(tile % share * 2 * GROUP, 2 * GROUP)
+                for g in range(groups):
+                    block = block_index(stages, g, low, tile // share)
+                    stream.sums[0][block, rows, :] = pair[g]
+            stream.start(0)
+
+    begin(2, terms2)
 
     @pl.when(me < spaces - 1)
     def _():
@@ -295,13 +348,16 @@
                 grad = (grad * slope_of(at)).astype(BF16).astype(F32)
                 gf[u, :, v, pl.ds(w, half_w, stride=2), :] = grad
 
-    red2.finish(0)
-
     grad = gf[...].reshape(-1, gf.shape[3], cells)
     grad_t = jnp.concatenate(
         [jnp.transpose(flat(grad)).astype(BF16), jnp.transpose(flat(shift_up(grad))).astype(BF16)],
         axis=0,
     )
+    early = [stream for stream, plan in zip(streams, plans) if plan[3] == 2]
+    late = [stream for stream, plan in zip(streams, plans) if plan[3] == 1]
+    for stream in early:
+        stream.finish(0)
+
     pairs1, lefts1 = [], []
     for a in range(3):
         columns = jnp.concatenate(
@@ -322,12 +378,22 @@
     for k in range(0, 9, 2):
         upper = lefts1[k + 1] if k + 1 < 9 else jnp.zeros_like(lefts1[k])
         pairs1.append(jnp.where(lane < half, pltpu.roll(lefts1[k], half, 1), upper))
-    store_terms(sums1[0], pairs1)
-    red1.start(0)
-    for t in range(count):
-        if t + 1 < count:
-            red2.finish(t + 1)
-        red1.finish(t)
+    begin(1, pairs1)
+    for stream in late:
+        stream.finish(0)
+    for t in range(1, max(len(stream.stages) for stream in streams)):
+        for stream in streams:
+            if t < len(stream.stages):
+                stream.finish(t)
+
+    for ab in range(9):
+        centre = sum1[pl.ds(ab * GROUP, GROUP), :]
+        side = sum1[pl.ds((9 + ab // 2) * GROUP, GROUP), :]
+        if ab % 2:
+            side = pltpu.roll(side, half, 1)
+        out1[3 * ab] = side[:, :half]
+        out1[3 * ab + 1] = centre[:, :half]
+        out1[3 * ab + 2] = pltpu.roll(centre, half, 1)[:, :half]
 
     @pl.when(me < spaces - 1)
     def _():
@@ -349,24 +415,27 @@
     _, _, q, r, _ = upstream_grad.shape
     up = upstream_grad.reshape(q * r, c1)
     groups = min(c1 // GROUP, spaces)
-    stages = stages_of(spaces, samples, groups)
+    by_space = straight(spaces, samples, groups)
+    by_samples = samples_early(spaces, samples, groups) if samples > 1 else by_space
+    plans = [(by_space, 6, 0, 2), (by_samples, 8, 6, 2), (by_space, 7, 0, 1)]
     rows2, rows1 = 28 * GROUP, 14 * GROUP
 
-    def buffers(rows):
-        sums, received, size = [], [], groups
-        for _, _, halves in stages:
+    def buffers(stages, tiles):
+        split = split_of(stages)
+        rows = tiles * 2 * GROUP // split
+        sums, received, size = [], [], groups * split
+        for _, _, kind in stages:
             sums.append(pltpu.VMEM((size, rows, c1), BF16))
-            size = size // 2 if halves else size
+            size = size // 2 if kind == "halve" else size
             received.append(pltpu.VMEM((size, rows, c1), BF16))
-        return sums + received
+        return sums + received + [pltpu.SemaphoreType.DMA((len(stages),))] * 2
 
     vmem = pl.BlockSpec(memory_space=pltpu.VMEM)
-    dmas = pltpu.SemaphoreType.DMA((len(stages),))
     second_out, out1, out2 = pl.pallas_call(
-        functools.partial(kernel, stages, spaces, groups),
+        functools.partial(kernel, plans, spaces, groups),
         out_shape=(
             jax.ShapeDtypeStruct((q * r, c1), BF16),
-            jax.ShapeDtypeStruct((rows1, c1), F32),
+            jax.ShapeDtypeStruct((27, GROUP, c0), F32),
             jax.ShapeDtypeStruct((rows2, c1), F32),
         ),
         in_specs=[vmem] * 4,
@@ -379,14 +448,10 @@
             pltpu.VMEM((q, r, c1), BF16),
             pltpu.VMEM((q, r, c1), BF16),
             pltpu.VMEM((2, height // 4, 2, width // 2, c1), F32),
+            pltpu.VMEM((rows1, c1), F32),
             pltpu.SemaphoreType.DMA((3,)),
             pltpu.SemaphoreType.DMA((3,)),
-            *buffers(rows2),
-            *buffers(rows1),
-            dmas,
-            dmas,
-            dmas,
-            dmas,
+            *[each for plan in plans for each in buffers(*plan[:2])],
         ],
         compiler_params=pltpu.CompilerParams(
             collective_id=0, has_side_effects=True, vmem_limit_bytes=50 * 1024 * 1024
@@ -396,15 +461,11 @@
     own = c1 // spaces
     start = (lax.axis_index("space") % (GROUP // own)) * own if own < GROUP else 0
     units2 = out2.reshape(28, GROUP, c1)[:27]
-    units1 = out1.reshape(14, GROUP, 2, c0)
     if own < GROUP:
         units2 = lax.dynamic_slice_in_dim(units2, start, own, 1)
-        units1 = lax.dynamic_slice_in_dim(units1, start, own, 1)
+        out1 = lax.dynamic_slice_in_dim(out1, start, own, 1)
     second_grad = units2.reshape(3, 3, 3, own, c1)
-    centre = jnp.transpose(units1[:9], (0, 2, 3, 1))
-    left = jnp.transpose(units1[9:], (0, 2, 3, 1)).reshape(10, c0, own)
-    left = left[:9]
-    first_grad = jnp.concatenate([left[:, None], centre], axis=1).reshape(3, 3, 3, c0, own)
+    first_grad = jnp.transpose(out1.reshape(3, 3, 3, own, c0), (0, 1, 2, 4, 3))
     return second_out.reshape(1, 1, q, r, c1), first_grad, second_grad
 
 

time: 40.4 us -> 37.4 us (0.926)
  Pallas kernels: 35.8 us -> 33.1 us
  other arithmetic: 0.66 us -> 0 us
  local copies, waits for them, and re-layouts: 3.04 us -> 3.47 us
    pallas_call x1, Pallas kernels: 35.8 us -> 33.1 us  [local(): pl.pallas_call(functools.partial(kernel, plans, spaces, groups), out_shap...]
    concatenate x1 -> x0, other arithmetic: 0.66 us -> none  [local(): jnp.concatenate([left[:, None], centre], axis=1).reshape(3, 3, 3, c0, own)]
    unnamed x8 -> x9, local copies, waits for them, and re-layouts: 2.17 us -> 2.82 us
where the time goes in v2:
time: 37.4 us; the launch traced here: 37.3 us
  Pallas kernels  33.1 us (89%)
  local copies, waits for them, and re-layouts  3.47 us (9%)
  between operations  0.7 us (2%)
    pallas_call x1, Pallas kernels, local(): pl.pallas_call(functools.partial(kernel, plans, spaces, groups), out_shap...  33.1 us
    unnamed x9, local copies, waits for them, and re-layouts  2.82 us

profile of v2, /device:TPU:0, one launch (start us, length us, event | category | flops | bytes accessed | tf_op | source)
XLA Modules:
  0.0 37.3 jit_solution(9453233119969332382)
XLA Ops:
  0.6 0.0 copy-start
  0.6 0.0 copy-start.1
  0.7 0.0 copy-start.2
  0.7 1.5 %copy.7 = bf16[16,8,32,128]{3,2,1,0:T(8,128)(2,1)S(1)} copy(bf16[16,8,32,128]{3,1,2,0:T(8,128)(2,1)} %bitcast.19) | data formatting | bytes 2097152
  2.2 0.0 copy-done
  2.2 0.0 copy-done.1
  2.2 0.0 copy-done.2
  2.2 33.1 %shard_map.67 = (bf16[128,128]{1,0:T(8,128)(2,1)S(1)}, f32[27,8,64]{2,1,0:T(8,128)S(1)}, f32[224,128]{1,0:T(8,128)S(1)}) custom-call(bf16[4,16,2,32,128]{4,3,2,1,0:T(8,128)(2,1)S(1)} %bitcast.13, bf16[27,64,128]{2,1,0:T(8,128)(2,1)S(1)} %bitcast.15, bf16[27,128,128]{2,1,0:T(8,128)(2,1)S(1)} %bitcast.14, bf16[128,128]{1,0:T(8,128)(2,1)S(1)} %bitcast.17), custom_call_target="tpu_custom_call" | custom-call | tf_op jit(solution)/shard_map/pallas_call | solution.py:434
  35.4 0.7 %slice.4 = f32[216,128]{1,0:T(8,128)} slice(f32[224,128]{1,0:T(8,128)S(1)} %get-tuple-element.8), slice={[0:216], [0:128]} | slice | bytes 221184 | tf_op jit(solution)/shard_map/slice | solution.py:463
  36.0 0.6 %copy.10 = bf16[1,1,8,16,128]{4,3,2,1,0:T(8,128)(2,1)} copy(bf16[1,1,8,16,128]{4,3,2,1,0:T(8,128)(2,1)S(1)} %bitcast.18) | data formatting | bytes 65536
  36.6 0.6 %copy.11 = f32[3,3,3,64,8]{3,4,2,1,0:T(8,128)} copy(f32[3,3,3,64,8]{3,4,2,1,0:T(8,128)S(1)} %bitcast.16) | data formatting | bytes 110592
Async XLA Ops:
  0.6 1.6 %copy-start = (bf16[3,3,3,128,128]{4,3,2,1,0:T(8,128)(2,1)S(1)}, bf16[3,3,3,128,128]{4,3,2,1,0:T(8,128)(2,1)}, u32[]{:S(2)}) copy-start(bf16[3,3,3,128,128]{4,3,2,1,0:T(8,128)(2,1)} %param.6) | copy-start | bytes 2654212
  0.6 1.6 %copy-start.1 = (bf16[3,3,3,64,128]{4,3,2,1,0:T(8,128)(2,1)S(1)}, bf16[3,3,3,64,128]{4,3,2,1,0:T(8,128)(2,1)}, u32[]{:S(2)}) copy-start(bf16[3,3,3,64,128]{4,3,2,1,0:T(8,128)(2,1)} %param.5) | copy-start | bytes 1327108
  0.7 1.6 %copy-start.2 = (bf16[1,1,8,16,128]{4,3,2,1,0:T(8,128)(2,1)S(1)}, bf16[1,1,8,16,128]{4,3,2,1,0:T(8,128)(2,1)}, u32[]{:S(2)}) copy-start(bf16[1,1,8,16,128]{4,3,2,1,0:T(8,128)(2,1)} %param.7) | copy-start | bytes 98308

commit v3 on v2

--- a/solution.py
+++ b/solution.py
@@ -26,8 +26,10 @@
     return list(range(extra, log2(spaces))), list(range(extra))
 
 
-def straight(spaces, samples, groups):
+def straight(spaces, samples, groups, crossed=False):
     halving, shared = bits_of(spaces, groups)
+    if crossed:
+        halving = halving[:1] + halving[2:3] + halving[1:2] + halving[3:]
     stages = [("space", k, "halve") for k in halving]
     stages += [("space", k, "full") for k in shared]
     return stages + [("dp", k, "full") for k in range(log2(samples))]
@@ -348,16 +350,16 @@
                 grad = (grad * slope_of(at)).astype(BF16).astype(F32)
                 gf[u, :, v, pl.ds(w, half_w, stride=2), :] = grad
 
+    early = [stream for stream, plan in zip(streams, plans) if plan[3] == 2]
+    late = [stream for stream, plan in zip(streams, plans) if plan[3] == 1]
+    for stream in early:
+        stream.finish(0)
+
     grad = gf[...].reshape(-1, gf.shape[3], cells)
     grad_t = jnp.concatenate(
         [jnp.transpose(flat(grad)).astype(BF16), jnp.transpose(flat(shift_up(grad))).astype(BF16)],
         axis=0,
     )
-    early = [stream for stream, plan in zip(streams, plans) if plan[3] == 2]
-    late = [stream for stream, plan in zip(streams, plans) if plan[3] == 1]
-    for stream in early:
-        stream.finish(0)
-
     pairs1, lefts1 = [], []
     for a in range(3):
         columns = jnp.concatenate(
@@ -381,10 +383,13 @@
     begin(1, pairs1)
     for stream in late:
         stream.finish(0)
-    for t in range(1, max(len(stream.stages) for stream in streams)):
-        for stream in streams:
+    for t in range(1, max(len(stream.stages) for stream in streams) + 1):
+        for stream in early:
             if t < len(stream.stages):
                 stream.finish(t)
+        for stream in late:
+            if 1 < t <= len(stream.stages):
+                stream.finish(t - 1)
 
     for ab in range(9):
         centre = sum1[pl.ds(ab * GROUP, GROUP), :]
@@ -417,7 +422,8 @@
     groups = min(c1 // GROUP, spaces)
     by_space = straight(spaces, samples, groups)
     by_samples = samples_early(spaces, samples, groups) if samples > 1 else by_space
-    plans = [(by_space, 6, 0, 2), (by_samples, 8, 6, 2), (by_space, 7, 0, 1)]
+    crossed = straight(spaces, samples, groups, True)
+    plans = [(by_space, 6, 0, 2), (by_samples, 8, 6, 2), (by_space, 4, 0, 1), (crossed, 3, 4, 1)]
     rows2, rows1 = 28 * GROUP, 14 * GROUP
 
     def buffers(stages, tiles):

time: 37.4 us -> 36 us (0.963)
  Pallas kernels: 33.1 us -> 31.7 us
    pallas_call x1, Pallas kernels: 33.1 us -> 31.7 us  [local(): pl.pallas_call(functools.partial(kernel, plans, spaces, groups), out_shap...]
where the time goes in v3:
time: 36 us; the launch traced here: 35.9 us
  Pallas kernels  31.7 us (88%)
  local copies, waits for them, and re-layouts  3.47 us (10%)
  between operations  0.7 us (2%)
    pallas_call x1, Pallas kernels, local(): pl.pallas_call(functools.partial(kernel, plans, spaces, groups), out_shap...  31.7 us
    unnamed x9, local copies, waits for them, and re-layouts  2.82 us

profile of v3, /device:TPU:0, one launch (start us, length us, event | category | flops | bytes accessed | tf_op | source)
XLA Modules:
  0.0 35.9 jit_solution(1779608927479922541)
XLA Ops:
  0.6 0.0 copy-start
  0.6 0.0 copy-start.1
  0.7 0.0 copy-start.2
  0.7 1.5 %copy.7 = bf16[16,8,32,128]{3,2,1,0:T(8,128)(2,1)S(1)} copy(bf16[16,8,32,128]{3,1,2,0:T(8,128)(2,1)} %bitcast.19) | data formatting | bytes 2097152
  2.2 0.0 copy-done
  2.2 0.0 copy-done.1
  2.2 0.0 copy-done.2
  2.2 31.7 %shard_map.67 = (bf16[128,128]{1,0:T(8,128)(2,1)S(1)}, f32[27,8,64]{2,1,0:T(8,128)S(1)}, f32[224,128]{1,0:T(8,128)S(1)}) custom-call(bf16[4,16,2,32,128]{4,3,2,1,0:T(8,128)(2,1)S(1)} %bitcast.13, bf16[27,64,128]{2,1,0:T(8,128)(2,1)S(1)} %bitcast.15, bf16[27,128,128]{2,1,0:T(8,128)(2,1)S(1)} %bitcast.14, bf16[128,128]{1,0:T(8,128)(2,1)S(1)} %bitcast.17), custom_call_target="tpu_custom_call" | custom-call | tf_op jit(solution)/shard_map/pallas_call | solution.py:440
  34.0 0.7 %slice.4 = f32[216,128]{1,0:T(8,128)} slice(f32[224,128]{1,0:T(8,128)S(1)} %get-tuple-element.8), slice={[0:216], [0:128]} | slice | bytes 221184 | tf_op jit(solution)/shard_map/slice | solution.py:469
  34.6 0.6 %copy.10 = bf16[1,1,8,16,128]{4,3,2,1,0:T(8,128)(2,1)} copy(bf16[1,1,8,16,128]{4,3,2,1,0:T(8,128)(2,1)S(1)} %bitcast.18) | data formatting | bytes 65536
  35.3 0.6 %copy.11 = f32[3,3,3,64,8]{3,4,2,1,0:T(8,128)} copy(f32[3,3,3,64,8]{3,4,2,1,0:T(8,128)S(1)} %bitcast.16) | data formatting | bytes 110592
Async XLA Ops:
  0.6 1.6 %copy-start = (bf16[3,3,3,128,128]{4,3,2,1,0:T(8,128)(2,1)S(1)}, bf16[3,3,3,128,128]{4,3,2,1,0:T(8,128)(2,1)}, u32[]{:S(2)}) copy-start(bf16[3,3,3,128,128]{4,3,2,1,0:T(8,128)(2,1)} %param.6) | copy-start | bytes 2654212
  0.6 1.6 %copy-start.1 = (bf16[3,3,3,64,128]{4,3,2,1,0:T(8,128)(2,1)S(1)}, bf16[3,3,3,64,128]{4,3,2,1,0:T(8,128)(2,1)}, u32[]{:S(2)}) copy-start(bf16[3,3,3,64,128]{4,3,2,1,0:T(8,128)(2,1)} %param.5) | copy-start | bytes 1327108
  0.7 1.6 %copy-start.2 = (bf16[1,1,8,16,128]{4,3,2,1,0:T(8,128)(2,1)S(1)}, bf16[1,1,8,16,128]{4,3,2,1,0:T(8,128)(2,1)}, u32[]{:S(2)}) copy-start(bf16[1,1,8,16,128]{4,3,2,1,0:T(8,128)(2,1)} %param.7) | copy-start | bytes 98308

commit v4 on v3

--- a/solution.py
+++ b/solution.py
@@ -137,11 +137,11 @@
 
 
 def kernel(plans, spaces, groups, vol, w1, w2, up, second_out, out1, out2, *scratch):
-    (vol_rim, hidden_send, hidden_rim, hf, g2_send, g2_next, gf, sum1, halo_send, halo_recv) = scratch[:10]
-    at, streams = 10, []
+    (vol_rim, hidden_send, hidden_rim, hf, g2_send, g2_next, gf, sum1, sum2, halo_send, halo_recv) = scratch[:11]
+    at, streams = 11, []
     for stages, tiles, first_tile, layer in plans:
         used = 2 * len(stages) + 2
-        target = out2 if layer == 2 else sum1
+        target = sum2 if layer == 2 else sum1
         streams.append(Reduction(stages, scratch[at : at + used], target, first_tile * 2 * GROUP))
         at += used
     low = log2(spaces) - log2(groups)
@@ -391,6 +391,7 @@
             if 1 < t <= len(stream.stages):
                 stream.finish(t - 1)
 
+    out2[...] = sum2[pl.ds(0, out2.shape[0]), :]
     for ab in range(9):
         centre = sum1[pl.ds(ab * GROUP, GROUP), :]
         side = sum1[pl.ds((9 + ab // 2) * GROUP, GROUP), :]
@@ -442,7 +443,7 @@
         out_shape=(
             jax.ShapeDtypeStruct((q * r, c1), BF16),
             jax.ShapeDtypeStruct((27, GROUP, c0), F32),
-            jax.ShapeDtypeStruct((rows2, c1), F32),
+            jax.ShapeDtypeStruct((27 * GROUP, c1), F32),
         ),
         in_specs=[vmem] * 4,
         out_specs=(vmem,) * 3,
@@ -455,6 +456,7 @@
             pltpu.VMEM((q, r, c1), BF16),
             pltpu.VMEM((2, height // 4, 2, width // 2, c1), F32),
             pltpu.VMEM((rows1, c1), F32),
+            pltpu.VMEM((rows2, c1), F32),
             pltpu.SemaphoreType.DMA((3,)),
             pltpu.SemaphoreType.DMA((3,)),
             *[each for plan in plans for each in buffers(*plan[:2])],
@@ -466,7 +468,7 @@
 
     own = c1 // spaces
     start = (lax.axis_index("space") % (GROUP // own)) * own if own < GROUP else 0
-    units2 = out2.reshape(28, GROUP, c1)[:27]
+    units2 = out2.reshape(27, GROUP, c1)
     if own < GROUP:
         units2 = lax.dynamic_slice_in_dim(units2, start, own, 1)
         out1 = lax.dynamic_slice_in_dim(out1, start, own, 1)

time: 36 us -> 36 us (level)
    slice x1 -> x0, local copies, waits for them, and re-layouts: 0.65 us -> none  [local(): units2 = out2.reshape(28, GROUP, c1)[:27]]
    unnamed x9 -> x10, local copies, waits for them, and re-layouts: 2.82 us -> 3.47 us
where the time goes in v4:
time: 36 us; the launch traced here: 35.9 us
  Pallas kernels  31.7 us (88%)
  local copies, waits for them, and re-layouts  3.47 us (10%)
  between operations  0.7 us (2%)
    pallas_call x1, Pallas kernels, local(): pl.pallas_call(functools.partial(kernel, plans, spaces, groups), out_shap...  31.7 us
    unnamed x10, local copies, waits for them, and re-layouts  3.47 us

profile of v4, /device:TPU:0, one launch (start us, length us, event | category | flops | bytes accessed | tf_op | source)
XLA Modules:
  0.0 35.9 jit_solution(2866967846107976624)
XLA Ops:
  0.6 0.0 copy-start
  0.6 0.0 copy-start.1
  0.7 0.0 copy-start.2
  0.7 1.5 %copy.7 = bf16[16,8,32,128]{3,2,1,0:T(8,128)(2,1)S(1)} copy(bf16[16,8,32,128]{3,1,2,0:T(8,128)(2,1)} %bitcast.20) | data formatting | bytes 2097152
  2.2 0.0 copy-done
  2.2 0.0 copy-done.1
  2.2 0.0 copy-done.2
  2.2 31.7 %shard_map.67 = (bf16[128,128]{1,0:T(8,128)(2,1)S(1)}, f32[27,8,64]{2,1,0:T(8,128)S(1)}, f32[216,128]{1,0:T(8,128)S(1)}) custom-call(bf16[4,16,2,32,128]{4,3,2,1,0:T(8,128)(2,1)S(1)} %bitcast.13, bf16[27,64,128]{2,1,0:T(8,128)(2,1)S(1)} %bitcast.15, bf16[27,128,128]{2,1,0:T(8,128)(2,1)S(1)} %bitcast.14, bf16[128,128]{1,0:T(8,128)(2,1)S(1)} %bitcast.18), custom_call_target="tpu_custom_call" | custom-call | tf_op jit(solution)/shard_map/pallas_call | solution.py:441
  34.0 0.6 %copy.11 = bf16[1,1,8,16,128]{4,3,2,1,0:T(8,128)(2,1)} copy(bf16[1,1,8,16,128]{4,3,2,1,0:T(8,128)(2,1)S(1)} %bitcast.19) | data formatting | bytes 65536
  34.6 0.6 %copy.12 = f32[3,3,3,64,8]{3,4,2,1,0:T(8,128)} copy(f32[3,3,3,64,8]{3,4,2,1,0:T(8,128)S(1)} %bitcast.17) | data formatting | bytes 110592
  35.3 0.6 %copy.13 = f32[3,3,3,8,128]{4,3,2,1,0:T(8,128)} copy(f32[3,3,3,8,128]{4,3,2,1,0:T(8,128)S(1)} %bitcast.16) | data formatting | bytes 221184
Async XLA Ops:
  0.6 1.6 %copy-start = (bf16[3,3,3,128,128]{4,3,2,1,0:T(8,128)(2,1)S(1)}, bf16[3,3,3,128,128]{4,3,2,1,0:T(8,128)(2,1)}, u32[]{:S(2)}) copy-start(bf16[3,3,3,128,128]{4,3,2,1,0:T(8,128)(2,1)} %param.6) | copy-start | bytes 2654212
  0.6 1.6 %copy-start.1 = (bf16[3,3,3,64,128]{4,3,2,1,0:T(8,128)(2,1)S(1)}, bf16[3,3,3,64,128]{4,3,2,1,0:T(8,128)(2,1)}, u32[]{:S(2)}) copy-start(bf16[3,3,3,64,128]{4,3,2,1,0:T(8,128)(2,1)} %param.5) | copy-start | bytes 1327108
  0.7 1.6 %copy-start.2 = (bf16[1,1,8,16,128]{4,3,2,1,0:T(8,128)(2,1)S(1)}, bf16[1,1,8,16,128]{4,3,2,1,0:T(8,128)(2,1)}, u32[]{:S(2)}) copy-start(bf16[1,1,8,16,128]{4,3,2,1,0:T(8,128)(2,1)} %param.7) | copy-start | bytes 98308
